TPU v7x, 32 devices: a whole 2x2x4 slice. The times are simulated.
32 devices in a mesh: seq: 16 (over z, y, core), head: 2 (over x).
Axes of the slice: x: 2, y: 2, z: 4, core: 2. Of those that a mesh axis runs over, the one named last changes fastest.
Arguments:
- volume: bfloat16 [8192, 64], P('seq'), may hold values from -6 to 6
- vox_mask: int32 [8192, 64], P('seq'), may hold values 0 or 1
- embed: bfloat16 [64, 1024], replicated, may hold values from -0.75 to 0.75
- w_qkv: bfloat16 [3, 1024, 1024], P(None, None, 'head'), may hold values from -5 to 5
- w_out: bfloat16 [1024, 1024], P(None, 'head'), may hold values from -0.1875 to 0.1875
- w_head: bfloat16 [1024, 64], replicated, may hold values from -0.1875 to 0.1875
Outputs:
- grad_qkv: float32 [3, 1024, 1024], P(None, 'seq', 'head')
- grad_out: float32 [1024, 1024], P('seq', 'head')
All inputs are finite; a program needn't handle non-finite values. No bound on the sum of `vox_mask` on one device may be relied on, other than what follows from the above.
Results may differ from a plain program's by a relative error of at most 0.0038.
Values may be sent and summed in bfloat16 or wider, within the bound.
No kernel may reach another device: no remote copies, remote signals or barrier semaphores. Data moves between devices by JAX's collectives and lax.ppermute only.
A program may use at most 64 MiB of HBM per device.

v0:
```python
import math
import jax
import jax.numpy as jnp
from jax import lax
from jax.sharding import PartitionSpec as P

D = 1024
HEADS = 16
LEVELS = 2


def partner(shard, axis, apart):
    return lax.ppermute(shard, axis, [(i, i ^ 1 << apart) for i in range(lax.axis_size(axis))])


def head_major(rows, head_dim):
    return rows.reshape(rows.shape[0], rows.shape[1] // head_dim, head_dim).transpose(1, 0, 2)


def token_major(blocks):
    return blocks.transpose(1, 0, 2).reshape(blocks.shape[1], blocks.shape[0] * blocks.shape[2])


def softmax_rows(query_head, key_head, factor):
    scores = (
        jnp.einsum("qd,kd->qk", query_head, key_head, preferred_element_type=jnp.float32) * factor
    )
    highest = jnp.max(scores, -1, keepdims=True)
    raised = jnp.exp(scores - highest)
    return raised / jnp.sum(raised, -1, keepdims=True)


def per_device(volume, vox_mask, embed, w_qkv, w_out, w_head):
    tok_rows = volume.shape[0]
    head_dim = D // HEADS
    factor = head_dim ** (-0.5)
    seq_devices = lax.axis_size("seq")
    kept = volume * (1 - vox_mask).astype(jnp.bfloat16)
    hidden = jnp.dot(kept, embed, preferred_element_type=jnp.float32)
    normed = (hidden * lax.rsqrt(jnp.mean(hidden * hidden, -1, keepdims=True) + 1e-06)).astype(
        jnp.bfloat16
    )
    projected = jnp.einsum("td,jdc->jtc", normed, w_qkv, preferred_element_type=jnp.float32).astype(
        jnp.bfloat16
    )
    remote = [partner(projected[1:], "seq", level_bit) for level_bit in range(LEVELS)]
    key_rows = jnp.concatenate([projected[1]] + [other[0] for other in remote], 0)
    value_rows = jnp.concatenate([projected[2]] + [other[1] for other in remote], 0)
    query_heads = head_major(projected[0], head_dim)
    key_heads = head_major(key_rows, head_dim)
    value_heads = head_major(value_rows, head_dim)

    def forward_head(operands):
        query_head, key_head, value_head = operands
        weights = softmax_rows(query_head, key_head, factor).astype(jnp.bfloat16)
        return jnp.dot(weights, value_head, preferred_element_type=jnp.float32).astype(jnp.bfloat16)

    context_heads = lax.map(forward_head, (query_heads, key_heads, value_heads))
    context = token_major(context_heads)
    partial_out = jnp.einsum("tc,oc->to", context, w_out, preferred_element_type=jnp.float32)
    mixed = lax.psum(partial_out.astype(jnp.bfloat16), "head").astype(jnp.float32)
    stream = (hidden + mixed).astype(jnp.bfloat16)
    predicted = jnp.dot(stream, w_head, preferred_element_type=jnp.float32)
    loss_weight = 256.0 / math.sqrt(tok_rows * seq_devices)
    grad_pred = (
        vox_mask.astype(jnp.float32) * (predicted - volume.astype(jnp.float32)) * loss_weight
    ).astype(jnp.bfloat16)
    grad_stream = jnp.einsum(
        "tv,dv->td", grad_pred, w_head, preferred_element_type=jnp.float32
    ).astype(jnp.bfloat16)
    grad_context = jnp.dot(grad_stream, w_out, preferred_element_type=jnp.float32).astype(
        jnp.bfloat16
    )

    def backward_head(operands):
        query_head, key_head, value_head, context_head, grad_head = operands
        probs = softmax_rows(query_head, key_head, factor)
        grad_probs = jnp.einsum(
            "qd,kd->qk", grad_head, value_head, preferred_element_type=jnp.float32
        )
        offsets = jnp.sum(
            grad_head.astype(jnp.float32) * context_head.astype(jnp.float32), -1, keepdims=True
        )
        grad_scores = (probs * (grad_probs - offsets) * factor).astype(jnp.bfloat16)
        grad_query = jnp.dot(grad_scores, key_head, preferred_element_type=jnp.float32).astype(
            jnp.bfloat16
        )
        grad_key = jnp.einsum(
            "qk,qd->kd", grad_scores, query_head, preferred_element_type=jnp.float32
        ).astype(jnp.bfloat16)
        grad_value = jnp.einsum(
            "qk,qd->kd", probs.astype(jnp.bfloat16), grad_head, preferred_element_type=jnp.float32
        ).astype(jnp.bfloat16)
        return (grad_query, grad_key, grad_value)

    grad_q_heads, grad_k_heads, grad_v_heads = lax.map(
        backward_head,
        (query_heads, key_heads, value_heads, context_heads, head_major(grad_context, head_dim)),
    )
    grad_query = token_major(grad_q_heads)
    local_width = grad_query.shape[1]
    blocks_all = LEVELS + 1
    grad_keys = token_major(grad_k_heads).reshape(blocks_all, tok_rows, local_width)
    grad_values = token_major(grad_v_heads).reshape(blocks_all, tok_rows, local_width)
    returned = [
        partner(jnp.stack([grad_keys[level_bit + 1], grad_values[level_bit + 1]]), "seq", level_bit)
        for level_bit in range(LEVELS)
    ]
    own_keys = jnp.stack([grad_keys[0]] + [other[0] for other in returned])
    own_values = jnp.stack([grad_values[0]] + [other[1] for other in returned])
    source = normed
    query_term = jnp.einsum("tr,tc->rc", source, grad_query, preferred_element_type=jnp.float32)
    source = normed
    key_term = jnp.einsum("tr,jtc->rc", source, own_keys, preferred_element_type=jnp.float32)
    value_term = jnp.einsum("tr,jtc->rc", source, own_values, preferred_element_type=jnp.float32)
    key_term, value_term = (key_term, value_term)
    out_term = jnp.einsum("tr,tc->rc", grad_stream, context, preferred_element_type=jnp.float32)
    summed = lax.psum_scatter(
        jnp.stack([query_term, key_term, value_term, out_term], 1),
        "seq",
        scatter_dimension=0,
        tiled=True,
    )
    return (jnp.transpose(summed[:, :3, :], (1, 0, 2)), summed[:, 3, :])


def solution(mesh):
    return jax.shard_map(
        per_device,
        mesh=mesh,
        in_specs=(P("seq", None), P("seq", None), P(), P(None, None, "head"), P(None, "head"), P()),
        out_specs=(P(None, "seq", "head"), P("seq", "head")),
        check_vma=False,
    )
```

profile of v0, /device:TPU:0, one launch (start us, length us, event | category | flops | bytes accessed | tf_op | source)
XLA Modules:
  0.0 395.8 jit_solution(14222275033119210577)
XLA Ops:
  13.9 2.5 collective-permute-start.1
  18.8 2.2 fusion.67
  22.6 17.9 %collective-permute-done.1 = bf16[2,512,512]{1,2,0:T(8,128)(2,1)} collective-permute-done((bf16[2,512,512]{1,2,0:T(8,128)(2,1)}, bf16[2,512,512]{1,2,0:T(8,128)(2,1)}, u32[]{:S(2)}, u32[]{:S(2)}) %collective-permute-start.1) | collective-permute-done | bytes 1048608 | tf_op jit(solution)/shard_map/ppermute | solution.py:13
  40.5 2.3 fusion.68
  42.8 2.4 copy.22
  45.2 2.3 copy.24
  47.5 2.4 copy.25
  49.9 4.6 %maximum_bitcast_fusion = (bf16[8,1536,64]{2,1,0:T(8,128)(2,1)}, bf16[8,1536,64]{2,1,0:T(8,128)(2,1)}) fusion(bf16[512,8,64]{2,0,1:T(8,128)(2,1)} %copy.22, bf16[512,8,64]{2,0,1:T(8,128)(2,1)S(1)} %copy.21, bf16[512,8,64]{2,0,1:T(8,128)(2,1)S(1)} %copy.20, bf16[512,8,64]{2,0,1:T(8,128)(2,1)} %copy.25, bf16[512,8,64]{2,0,1:T(8,128)(2,1)} %copy.24, ...), kind=kLoop, calls=%fused_computation.57 | loop fusion | flops 9437184 | bytes 6291456 | tf_op jit(solution)/shard_map/transpose | solution.py:17
  55.3 37.6 %while.24 = (s32[]{:T(128)}, bf16[8,512,64]{1,2,0:T(8,128)(2,1)}, bf16[8,512,64]{2,1,0:T(8,128)(2,1)}, bf16[8,1536,64]{2,1,0:T(8,128)(2,1)}, bf16[8,1536,64]{2,1,0:T(8,128)(2,1)}, /*index=5*/s32[]{:T(128)}) while((s32[]{:T(128)}, bf16[8,512,64]{1,2,0:T(8,128)(2,1)}, bf16[8,512,64]{2,1,0:T(8,128)(2,1)}, bf16[8,1536,64]{2,1,0:T(8,128)(2,1)}, ...), condition=%wide.region_4.5_spmd, body=%wide.region_1.4_spmd.sunk | while | flops 206863360 | bytes 10432581 | solution.py:58
  57.6 2.4 fusion.109
  62.3 2.4 fusion.109
  67.0 2.4 fusion.109
  71.7 2.4 fusion.109
  76.4 2.4 fusion.109
  81.1 2.4 fusion.109
  85.8 2.4 fusion.109
  90.5 2.4 fusion.109
  92.9 3.3 convolution_convert_fusion.5
  96.5 41.5 %all-reduce.2.cloned.1.call-done = bf16[512,1024]{1,0:T(8,128)(2,1)} async-done(((bf16[512,1024]{1,0:T(8,128)(2,1)}), bf16[512,1024]{1,0:T(8,128)(2,1)}) %all-reduce.2.cloned.1.call-update) | async-done | bytes 1048592 | tf_op jit(solution)/shard_map/psum | solution.py:61
  140.1 2.4 convolution_convert_fusion.6
  144.7 103.3 %while.25 = (s32[]{:T(128)}, bf16[8,512,64]{1,2,0:T(8,128)(2,1)}, bf16[8,1536,64]{1,2,0:T(8,128)(2,1)}, bf16[8,1536,64]{1,2,0:T(8,128)(2,1)}, bf16[8,512,64]{2,1...) while((s32[]{:T(128)}, bf16[8,512,64]{1,2,0:T(8,128)(2,1)}, ...), condition=%wide.region_10.11_spmd, body=%wide.region_6.10_spmd.sunk | while | flops 513899008 | bytes 19881068 | solution.py:96
  147.0 2.3 fusion.124
  159.9 2.3 fusion.124
  172.8 2.3 fusion.124
  185.7 2.3 fusion.124
  198.6 2.3 fusion.124
  211.6 2.3 fusion.124
  224.5 2.3 fusion.124
  237.4 2.3 fusion.124
  255.5 20.4 %collective-permute-done.3 = bf16[2,512,512]{1,2,0:T(8,128)(2,1)S(1)} collective-permute-done((bf16[2,512,512]{1,2,0:T(8,128)(2,1)S(1)}, bf16[2,512,512]{1,2,0:T(8,128)(2,1)S(1)}, u32[]{:S(2)}, u32[]{:S(2)}) %collective-permute-start.3) | collective-permute-done | bytes 1048608 | tf_op jit(solution)/shard_map/ppermute | solution.py:13
  278.0 4.0 pad_maximum_fusion
  282.0 103.6 %reduce-scatter.2.cloned.1.call-done = f32[64,4,512]{2,0,1:T(8,128)} async-done(((f32[1024,4,512]{2,0,1:T(8,128)}), f32[64,4,512]{2,0,1:T(8,128)}) %reduce-scatter.2.cloned.1.call-update) | async-done | bytes 524304 | tf_op jit(solution)/shard_map/reduce_scatter | solution.py:118
  (143 shorter events, 131.6 us)
Async XLA Ops:
  7.2 3.3 copy-start
  7.2 130.8 %all-reduce.2.cloned.1.call-start = ((), (), s32[]{:S(2)}) async-start(), calls=%async_computation.1 | async-start | bytes 2097152 | tf_op jit(solution)/shard_map/psum | solution.py:61
  8.9 1.4 copy-start.2
  10.5 1.9 copy-start.4
  13.4 5.4 %collective-permute-start = (bf16[2,512,512]{1,2,0:T(8,128)(2,1)}, bf16[2,512,512]{1,2,0:T(8,128)(2,1)}, u32[]{:S(2)}, u32[]{:S(2)}) collective-permute-start(bf16[2,512,512]{1,2,0:T(8,128)(2,1)} %slice.107), channel_id=1, source_target_pairs={{0,2},{2,0},{4,6},{6,4},{8,10},{10,8},{12,14},{14,12},{16,18},{18,... | collective-permute-start | bytes 3145736 | tf_op jit(solution)/shard_map/ppermute | solution.py:13
  13.9 26.6 %collective-permute-start.1 = (bf16[2,512,512]{1,2,0:T(8,128)(2,1)}, bf16[2,512,512]{1,2,0:T(8,128)(2,1)}, u32[]{:S(2)}, u32[]{:S(2)}) collective-permute-start(bf16[2,512,512]{1,2,0:T(8,128)(2,1)} %slice.107), channel_id=1, source_target_pairs={{0,4},{2,6},{4,0},{6,2},{8,12},{10,14},{12,8},{14,10},{16,20},{18,... | collective-permute-start | bytes 3145736 | tf_op jit(solution)/shard_map/ppermute | solution.py:13
  92.9 45.1 %copy-start.3 = (f32[512,1024]{1,0:T(8,128)S(1)}, f32[512,1024]{1,0:T(8,128)}, u32[]{:S(2)}) copy-start(f32[512,1024]{1,0:T(8,128)} %copy-done.2) | copy-start | bytes 6291460
  92.9 45.1 %copy-start.9 = (s32[512,64]{0,1:T(8,128)S(1)}, s32[512,64]{0,1:T(8,128)}, u32[]{:S(2)}) copy-start(s32[512,64]{0,1:T(8,128)} %param.11) | copy-start | bytes 393220
  92.9 45.1 %copy-start.10 = (bf16[1024,64]{0,1:T(8,128)(2,1)S(1)}, bf16[1024,64]{0,1:T(8,128)(2,1)}, u32[]{:S(2)}) copy-start(bf16[1024,64]{0,1:T(8,128)(2,1)} %param.15) | copy-start | bytes 393220
  92.9 45.1 %copy-start.11 = (bf16[512,64]{0,1:T(8,128)(2,1)S(1)}, bf16[512,64]{0,1:T(8,128)(2,1)}, u32[]{:S(2)}) copy-start(bf16[512,64]{0,1:T(8,128)(2,1)} %param.10) | copy-start | bytes 196612
  96.3 289.3 %reduce-scatter.2.cloned.1.call-start = ((), (), s32[]{:S(2)}) async-start(), calls=%async_computation.2 | async-start | bytes 8912896 | tf_op jit(solution)/shard_map/reduce_scatter | solution.py:118
  140.1 4.6 %copy-start.6 = (bf16[512,1024]{1,0:T(8,128)(2,1)}, bf16[512,1024]{1,0:T(8,128)(2,1)S(1)}, u32[]{:S(2)}) copy-start(bf16[512,1024]{1,0:T(8,128)(2,1)S(1)} %convolution_convert_fusion.4) | copy-start | bytes 3145732
  248.0 1.9 copy-start.8
  249.9 2.0 copy-start.7
  250.1 3.6 copy-start.5
  250.1 5.4 %collective-permute-start.2 = (bf16[2,512,512]{1,2,0:T(8,128)(2,1)S(1)}, bf16[2,512,512]{1,2,0:T(8,128)(2,1)S(1)}, u32[]{:S(2)}, u32[]{:S(2)}) collective-permute-start(bf16[2,512,512]{1,2,0:T(8,128)(2,1)S(1)} %pad_maximum_fusion.1), channel_id=1, source_target_pairs={{0,2},{2,0},{4,6},{6,4},{8,10},{10,8},{12,14},{14,12},{16,18},{18,... | collective-permute-start | bytes 3145736 | tf_op jit(solution)/shard_map/ppermute | solution.py:13
  250.3 25.6 %collective-permute-start.3 = (bf16[2,512,512]{1,2,0:T(8,128)(2,1)S(1)}, bf16[2,512,512]{1,2,0:T(8,128)(2,1)S(1)}, u32[]{:S(2)}, u32[]{:S(2)}) collective-permute-start(bf16[2,512,512]{1,2,0:T(8,128)(2,1)S(1)} %pad_maximum_fusion.2), channel_id=1, source_target_pairs={{0,4},{2,6},{4,0},{6,2},{8,12},{10,14},{12,8},{14,10},{16,20},{18,... | collective-permute-start | bytes 3145736 | tf_op jit(solution)/shard_map/ppermute | solution.py:13
  282.0 107.0 %copy-start.1 = (bf16[3,1024,512]{2,1,0:T(8,128)(2,1)S(1)}, bf16[3,1024,512]{2,1,0:T(8,128)(2,1)}, u32[]{:S(2)}) copy-start(bf16[3,1024,512]{2,1,0:T(8,128)(2,1)} %param.13) | copy-start | bytes 9437188
Sparse Core Ops, SparseCore 0:
  96.4 41.5 all-reduce.1
  282.1 103.4 reduce-scatter.1
where the time goes:
time: 398 us; the launch traced here: 396 us
  waiting for transfers between devices  183 us (46%)
  matrix products  132 us (33%)
  local copies, waits for them, and re-layouts  34.2 us (9%)
  other arithmetic  27 us (7%)
  between operations  14.3 us (4%)
  starting transfers between devices  4.87 us (1%)
    reduce_scatter x1, waiting for transfers between devices, per_device(): lax.psum_scatter(jnp.stack([query_term, key_term, value_term, out_term],...  104 us
    psum x1, waiting for transfers between devices, per_device(): lax.psum(partial_out.astype(jnp.bfloat16), 'head').astype(jnp.float32)  41.5 us
    ppermute x4, waiting for transfers between devices, partner(): lax.ppermute(shard, axis, [(i, i ^ 1 << apart) for i in range(lax.axis_si...  38.3 us
    dot_general x16, matrix products, softmax_rows(): jnp.einsum('qd,kd->qk', query_head, key_head, preferred_element_type=jnp....  27.6 us
    dot_general x8, matrix products, forward_head(): jnp.dot(weights, value_head, preferred_element_type=jnp.float32)  19.2 us
    dot_general x8, matrix products, backward_head(): jnp.einsum('qk,qd->kd', probs.astype(jnp.bfloat16), grad_head, preferred_...  18.7 us
    dot_general x8, matrix products, backward_head(): jnp.dot(grad_scores, key_head, preferred_element_type=jnp.float32)  17.7 us
    dot_general x8, matrix products, backward_head(): jnp.einsum('qk,qd->kd', grad_scores, query_head, preferred_element_type=j...  16.2 us
  transfers between devices with their start and end apart: 6, of which 4 were waited for; matrix products, arithmetic and copies ran while one was open for 3% of the time, Pallas kernels for 0%

commit v1 on v0

--- a/solution.py
+++ b/solution.py
@@ -7,6 +7,12 @@
 D = 1024
 HEADS = 16
 LEVELS = 2
+
+
+def gather_and_add(value, mesh_axis):
+    pieces = lax.all_gather(value, mesh_axis, axis=0, tiled=False)
+    total = pieces.sum(axis=0)
+    return total
 
 
 def partner(shard, axis, apart):
@@ -58,7 +64,7 @@
     context_heads = lax.map(forward_head, (query_heads, key_heads, value_heads))
     context = token_major(context_heads)
     partial_out = jnp.einsum("tc,oc->to", context, w_out, preferred_element_type=jnp.float32)
-    mixed = lax.psum(partial_out.astype(jnp.bfloat16), "head").astype(jnp.float32)
+    mixed = gather_and_add(partial_out.astype(jnp.bfloat16), "head").astype(jnp.float32)
     stream = (hidden + mixed).astype(jnp.bfloat16)
     predicted = jnp.dot(stream, w_head, preferred_element_type=jnp.float32)
     loss_weight = 256.0 / math.sqrt(tok_rows * seq_devices)

time: 398 us -> 395 us (level)
  waiting for transfers between devices: 183 us -> 176 us
    psum x1 -> x0, waiting for transfers between devices: 41.5 us -> none  [per_device(): lax.psum(partial_out.astype(jnp.bfloat16), 'head').astype(jnp.float32)]
    all_gather x0 -> x1, waiting for transfers between devices: none -> 34.5 us  [gather_and_add(): pieces = lax.all_gather(value, mesh_axis, axis=0, tiled=False)]
where the time goes in v1:
time: 395 us; the launch traced here: 392 us
  waiting for transfers between devices  176 us (45%)
  matrix products  132 us (33%)
  local copies, waits for them, and re-layouts  34.2 us (9%)
  other arithmetic  30.3 us (8%)
  between operations  14.3 us (4%)
  starting transfers between devices  4.87 us (1%)
    reduce_scatter x1, waiting for transfers between devices, per_device(): lax.psum_scatter(jnp.stack([query_term, key_term, value_term, out_term],...  104 us
    ppermute x4, waiting for transfers between devices, partner(): lax.ppermute(shard, axis, [(i, i ^ 1 << apart) for i in range(lax.axis_si...  38.3 us
    all_gather x1, waiting for transfers between devices, gather_and_add(): pieces = lax.all_gather(value, mesh_axis, axis=0, tiled=False)  34.5 us
    dot_general x16, matrix products, softmax_rows(): jnp.einsum('qd,kd->qk', query_head, key_head, preferred_element_type=jnp....  27.6 us
    dot_general x8, matrix products, forward_head(): jnp.dot(weights, value_head, preferred_element_type=jnp.float32)  19.3 us
    dot_general x8, matrix products, backward_head(): jnp.einsum('qk,qd->kd', probs.astype(jnp.bfloat16), grad_head, preferred_...  18.8 us
    dot_general x8, matrix products, backward_head(): jnp.dot(grad_scores, key_head, preferred_element_type=jnp.float32)  17.7 us
    dot_general x8, matrix products, backward_head(): jnp.einsum('qk,qd->kd', grad_scores, query_head, preferred_element_type=j...  16.1 us
  transfers between devices with their start and end apart: 6, of which 4 were waited for; matrix products, arithmetic and copies ran while one was open for 3% of the time, Pallas kernels for 0%

profile of v1, /device:TPU:0, one launch (start us, length us, event | category | flops | bytes accessed | tf_op | source)
XLA Modules:
  0.0 392.2 jit_solution(2212269871810560026)
XLA Ops:
  13.9 2.5 collective-permute-start.1
  22.6 17.9 %collective-permute-done.1 = bf16[2,512,512]{1,2,0:T(8,128)(2,1)} collective-permute-done((bf16[2,512,512]{1,2,0:T(8,128)(2,1)}, bf16[2,512,512]{1,2,0:T(8,128)(2,1)}, u32[]{:S(2)}, u32[]{:S(2)}) %collective-permute-start.1) | collective-permute-done | bytes 1048608 | tf_op jit(solution)/shard_map/ppermute | solution.py:19
  40.5 2.3 fusion.68
  42.8 2.4 copy.22
  45.2 2.3 copy.24
  47.6 2.4 copy.25
  49.9 4.6 %maximum_bitcast_fusion = (bf16[8,1536,64]{2,1,0:T(8,128)(2,1)}, bf16[8,1536,64]{2,1,0:T(8,128)(2,1)}) fusion(bf16[512,8,64]{2,0,1:T(8,128)(2,1)} %copy.22, bf16[512,8,64]{2,0,1:T(8,128)(2,1)S(1)} %copy.21, bf16[512,8,64]{2,0,1:T(8,128)(2,1)S(1)} %copy.20, bf16[512,8,64]{2,0,1:T(8,128)(2,1)} %copy.25, bf16[512,8,64]{2,0,1:T(8,128)(2,1)} %copy.24, ...), kind=kLoop, calls=%fused_computation.57 | loop fusion | flops 9437184 | bytes 6291456 | tf_op jit(solution)/shard_map/transpose | solution.py:23
  55.4 37.6 %while.24 = (s32[]{:T(128)}, bf16[8,512,64]{1,2,0:T(8,128)(2,1)}, bf16[8,512,64]{2,1,0:T(8,128)(2,1)}, bf16[8,1536,64]{2,1,0:T(8,128)(2,1)}, bf16[8,1536,64]{2,1,0:T(8,128)(2,1)}, /*index=5*/s32[]{:T(128)}) while((s32[]{:T(128)}, bf16[8,512,64]{1,2,0:T(8,128)(2,1)}, bf16[8,512,64]{2,1,0:T(8,128)(2,1)}, bf16[8,1536,64]{2,1,0:T(8,128)(2,1)}, ...), condition=%wide.region_4.5_spmd, body=%wide.region_1.4_spmd.sunk | while | flops 206863360 | bytes 10432581 | solution.py:64
  57.7 2.4 fusion.109
  62.4 2.4 fusion.109
  67.1 2.4 fusion.109
  71.8 2.4 fusion.109
  76.5 2.4 fusion.109
  81.2 2.4 fusion.109
  85.9 2.4 fusion.109
  90.6 2.4 fusion.109
  93.0 3.3 convolution_convert_fusion.5
  96.6 34.5 %all-gather.3.cloned.1.call-done = bf16[1024,1024]{1,0:T(8,128)(2,1)} async-done(((bf16[512,1024]{1,0:T(8,128)(2,1)}), bf16[1024,1024]{1,0:T(8,128)(2,1)}) %all-gather.3.cloned.1.call-update) | async-done | bytes 2097168 | tf_op jit(solution)/shard_map/all_gather | solution.py:13
  131.0 3.3 reduce_sum.67
  136.5 2.4 convolution_convert_fusion.6
  141.1 103.3 %while.25 = (s32[]{:T(128)}, bf16[8,512,64]{1,2,0:T(8,128)(2,1)}, bf16[8,1536,64]{1,2,0:T(8,128)(2,1)}, bf16[8,1536,64]{1,2,0:T(8,128)(2,1)}, bf16[8,512,64]{2,1...) while((s32[]{:T(128)}, bf16[8,512,64]{1,2,0:T(8,128)(2,1)}, ...), condition=%wide.region_10.11_spmd, body=%wide.region_6.10_spmd.sunk | while | flops 513899008 | bytes 19881068 | solution.py:102
  143.4 2.3 fusion.124
  156.3 2.3 fusion.124
  169.2 2.3 fusion.124
  182.2 2.3 fusion.124
  195.1 2.4 fusion.124
  208.0 2.3 fusion.124
  220.9 2.4 fusion.124
  233.8 2.3 fusion.124
  252.0 20.4 %collective-permute-done.3 = bf16[2,512,512]{1,2,0:T(8,128)(2,1)S(1)} collective-permute-done((bf16[2,512,512]{1,2,0:T(8,128)(2,1)S(1)}, bf16[2,512,512]{1,2,0:T(8,128)(2,1)S(1)}, u32[]{:S(2)}, u32[]{:S(2)}) %collective-permute-start.3) | collective-permute-done | bytes 1048608 | tf_op jit(solution)/shard_map/ppermute | solution.py:19
  274.4 4.0 %pad_maximum_fusion = f32[1024,4,512]{2,0,1:T(8,128)} fusion(f32[1024,1,512]{2,0,1:T(8,128)S(1)} %convolution_bitcast_fusion, f32[1024,1,512]{2,0,1:T(8,128)S(1)} %convolution_bitcast_fusion.2, f32[1024,1,512]{2,0,1:T(8,128)S(1)} %convolution_bitcast_fusion.3, f32[1024,1,512]{2,0,1:T(8,128)S(1)} %convolution_bitcast_fusion.1), kind=kLoop, calls=%fused_computation.56 | loop fusion | flops 6291456 | bytes 16777216 | tf_op jit(solution)/shard_map/stack | solution.py:125
  278.4 103.6 %reduce-scatter.2.cloned.1.call-done = f32[64,4,512]{2,0,1:T(8,128)} async-done(((f32[1024,4,512]{2,0,1:T(8,128)}), f32[64,4,512]{2,0,1:T(8,128)}) %reduce-scatter.2.cloned.1.call-update) | async-done | bytes 524304 | tf_op jit(solution)/shard_map/reduce_scatter | solution.py:124
  (144 shorter events, 133.9 us)
Async XLA Ops:
  7.2 3.3 copy-start
  7.2 123.9 %all-gather.3.cloned.1.call-start = ((), (), s32[]{:S(2)}) async-start(), calls=%async_computation.2 | async-start | bytes 3145728 | tf_op jit(solution)/shard_map/all_gather | solution.py:13
  8.9 1.4 copy-start.2
  10.5 1.9 copy-start.4
  13.4 5.4 %collective-permute-start = (bf16[2,512,512]{1,2,0:T(8,128)(2,1)}, bf16[2,512,512]{1,2,0:T(8,128)(2,1)}, u32[]{:S(2)}, u32[]{:S(2)}) collective-permute-start(bf16[2,512,512]{1,2,0:T(8,128)(2,1)} %slice.107), channel_id=1, source_target_pairs={{0,2},{2,0},{4,6},{6,4},{8,10},{10,8},{12,14},{14,12},{16,18},{18,... | collective-permute-start | bytes 3145736 | tf_op jit(solution)/shard_map/ppermute | solution.py:19
  13.9 26.6 %collective-permute-start.1 = (bf16[2,512,512]{1,2,0:T(8,128)(2,1)}, bf16[2,512,512]{1,2,0:T(8,128)(2,1)}, u32[]{:S(2)}, u32[]{:S(2)}) collective-permute-start(bf16[2,512,512]{1,2,0:T(8,128)(2,1)} %slice.107), channel_id=1, source_target_pairs={{0,4},{2,6},{4,0},{6,2},{8,12},{10,14},{12,8},{14,10},{16,20},{18,... | collective-permute-start | bytes 3145736 | tf_op jit(solution)/shard_map/ppermute | solution.py:19
  93.0 41.4 %copy-start.3 = (f32[512,1024]{1,0:T(8,128)S(1)}, f32[512,1024]{1,0:T(8,128)}, u32[]{:S(2)}) copy-start(f32[512,1024]{1,0:T(8,128)} %copy-done.2) | copy-start | bytes 6291460
  93.0 41.4 %copy-start.9 = (s32[512,64]{0,1:T(8,128)S(1)}, s32[512,64]{0,1:T(8,128)}, u32[]{:S(2)}) copy-start(s32[512,64]{0,1:T(8,128)} %param.11) | copy-start | bytes 393220
  93.0 41.4 %copy-start.10 = (bf16[1024,64]{0,1:T(8,128)(2,1)S(1)}, bf16[1024,64]{0,1:T(8,128)(2,1)}, u32[]{:S(2)}) copy-start(bf16[1024,64]{0,1:T(8,128)(2,1)} %param.15) | copy-start | bytes 393220
  93.0 41.4 %copy-start.11 = (bf16[512,64]{0,1:T(8,128)(2,1)S(1)}, bf16[512,64]{0,1:T(8,128)(2,1)}, u32[]{:S(2)}) copy-start(bf16[512,64]{0,1:T(8,128)(2,1)} %param.10) | copy-start | bytes 196612
  96.3 285.7 %reduce-scatter.2.cloned.1.call-start = ((), (), s32[]{:S(2)}) async-start(), calls=%async_computation.1 | async-start | bytes 8912896 | tf_op jit(solution)/shard_map/reduce_scatter | solution.py:124
  136.5 4.6 %copy-start.6 = (bf16[512,1024]{1,0:T(8,128)(2,1)}, bf16[512,1024]{1,0:T(8,128)(2,1)S(1)}, u32[]{:S(2)}) copy-start(bf16[512,1024]{1,0:T(8,128)(2,1)S(1)} %convolution_convert_fusion.4) | copy-start | bytes 3145732
  244.4 1.9 copy-start.8
  246.3 2.0 copy-start.7
  246.5 3.5 copy-start.5
  246.5 5.4 %collective-permute-start.2 = (bf16[2,512,512]{1,2,0:T(8,128)(2,1)S(1)}, bf16[2,512,512]{1,2,0:T(8,128)(2,1)S(1)}, u32[]{:S(2)}, u32[]{:S(2)}) collective-permute-start(bf16[2,512,512]{1,2,0:T(8,128)(2,1)S(1)} %pad_maximum_fusion.1), channel_id=1, source_target_pairs={{0,2},{2,0},{4,6},{6,4},{8,10},{10,8},{12,14},{14,12},{16,18},{18,... | collective-permute-start | bytes 3145736 | tf_op jit(solution)/shard_map/ppermute | solution.py:19
  246.7 25.6 %collective-permute-start.3 = (bf16[2,512,512]{1,2,0:T(8,128)(2,1)S(1)}, bf16[2,512,512]{1,2,0:T(8,128)(2,1)S(1)}, u32[]{:S(2)}, u32[]{:S(2)}) collective-permute-start(bf16[2,512,512]{1,2,0:T(8,128)(2,1)S(1)} %pad_maximum_fusion.2), channel_id=1, source_target_pairs={{0,4},{2,6},{4,0},{6,2},{8,12},{10,14},{12,8},{14,10},{16,20},{18,... | collective-permute-start | bytes 3145736 | tf_op jit(solution)/shard_map/ppermute | solution.py:19
  278.4 107.0 %copy-start.1 = (bf16[3,1024,512]{2,1,0:T(8,128)(2,1)S(1)}, bf16[3,1024,512]{2,1,0:T(8,128)(2,1)}, u32[]{:S(2)}) copy-start(bf16[3,1024,512]{2,1,0:T(8,128)(2,1)} %param.13) | copy-start | bytes 9437188
Sparse Core Ops, SparseCore 0:
  96.4 34.5 all-gather.2
  278.5 103.4 reduce-scatter.1
